TPU v7x, 32 devices: a whole 2x2x4 slice. The times are simulated.
32 devices in a mesh: head: 2 (over y), seq: 16 (over z, x, core).
Axes of the slice: x: 2, y: 2, z: 4, core: 2. Of those that a mesh axis runs over, the one named last changes fastest.
Arguments:
- queries: bfloat16 [16, 1024, 4096], P('seq', 'head'), may hold values from -6 to 6
- key_rows: bfloat16 [16, 1024, 4096], P('seq', 'head'), may hold values from -6 to 6
- value_rows: bfloat16 [16, 1024, 4096], P('seq', 'head'), may hold values from -6 to 6
- head_gain: float32 [4096], replicated, may hold values from 0.5 to 1.5
Outputs:
- attended: bfloat16 [16, 1024, 4096], P('seq', 'head')
All inputs are finite; a program needn't handle non-finite values.
Results may differ from a plain program's by a relative error of at most 0.0065.
Values may be sent and summed in bfloat16 or wider, within the bound.
A program may use at most 128 MiB of HBM per device.

v0:
```python
import jax
import jax.numpy as jnp
from jax import lax
from jax.sharding import PartitionSpec as P

DH = 128
BLOCK = 512


epsilon = 1e-06


def prefix_2(part, axis, combine, identity):
    place = lax.axis_index(axis)
    gathered = lax.all_gather(part, axis)
    state = jnp.zeros_like(part) + jnp.asarray(identity, part.dtype)

    def one(lap, state):
        return combine(state, lax.dynamic_index_in_dim(gathered, lap, 0, False))

    return lax.fori_loop(0, place, one, state)


def activate(rows):
    return jax.nn.silu(rows.astype(jnp.float32)).astype(jnp.bfloat16)


def add_states(earlier, later):
    return earlier + later


def attend(pieces, chain):
    moved_q, moved_k, moved_v = pieces
    row_count = moved_q.shape[0]
    head_count = moved_q.shape[2]
    head_width = moved_q.shape[3]
    blocks = row_count // BLOCK
    block_q = moved_q.reshape(blocks, BLOCK, head_count, head_width)
    block_k = moved_k.reshape(blocks, BLOCK, head_count, head_width)
    block_v = moved_v.reshape(blocks, BLOCK, head_count, head_width)
    states = jnp.einsum("nbhd,nbhe->nhde", block_k, block_v, preferred_element_type=jnp.float32)
    span_total = jnp.sum(states, axis=0)
    incoming = chain(span_total)
    running = jnp.cumsum(states, axis=0)
    exclusive = jnp.concatenate([jnp.zeros_like(states[:1]), running[:-1]], axis=0)
    prefix = incoming[None] + exclusive
    scores = jnp.einsum("nihd,njhd->nhij", block_q, block_k, preferred_element_type=jnp.float32)
    row_pos = lax.broadcasted_iota(jnp.int32, (BLOCK, BLOCK), 0)
    col_pos = lax.broadcasted_iota(jnp.int32, (BLOCK, BLOCK), 1)
    scores = jnp.where(row_pos >= col_pos, scores, 0.0).astype(jnp.bfloat16)
    local_part = jnp.einsum("nhij,njhe->nihe", scores, block_v, preferred_element_type=jnp.float32)
    carried = jnp.einsum(
        "nihd,nhde->nihe", block_q.astype(jnp.float32), prefix, precision=lax.Precision.HIGHEST
    )
    results = (local_part + carried).reshape(row_count, 1, head_count, head_width)
    normed = results * lax.rsqrt(jnp.mean(results * results, axis=-1, keepdims=True) + epsilon)
    return normed.astype(jnp.bfloat16)


def local(queries, key_rows, value_rows, head_gain):
    local_rows = queries.shape[1]
    groups = lax.axis_size("head")
    head_width = DH
    per_group = queries.shape[2] // (groups * head_width)
    shape_four = (local_rows, groups, per_group, head_width)
    act_q = activate(queries[0]).reshape(shape_four)
    act_k = activate(key_rows[0]).reshape(shape_four)
    plain_v = value_rows[0].reshape(shape_four)

    def chain_items(span_total):
        return prefix_2(span_total, "seq", add_states, jnp.zeros_like(span_total))

    normed = attend(
        (
            lax.all_to_all(act_q, "head", split_axis=1, concat_axis=0, tiled=True),
            lax.all_to_all(act_k, "head", split_axis=1, concat_axis=0, tiled=True),
            lax.all_to_all(plain_v, "head", split_axis=1, concat_axis=0, tiled=True),
        ),
        chain_items,
    )
    restored = lax.all_to_all(normed, "head", split_axis=0, concat_axis=1, tiled=True)
    flat = restored.reshape(local_rows, groups * per_group * head_width)
    attended = (flat.astype(jnp.float32) * head_gain[None, :]).astype(jnp.bfloat16)
    return attended.reshape(1, local_rows, flat.shape[1])


def solution(mesh):
    placed = (P("seq", "head", None), P("seq", "head", None), P("seq", "head", None), P())
    return jax.shard_map(
        local, mesh=mesh, in_specs=placed, out_specs=P("seq", "head", None), check_vma=False
    )
```

profile of v0, /device:TPU:27, one launch (start us, length us, event | category | flops | bytes accessed | tf_op | source)
XLA Modules:
  0.0 387.3 jit_solution(15479746537734423456)
XLA Ops:
  6.5 6.4 %copy.59 = bf16[1,512,4096]{1,2,0:T(8,128)(2,1)} copy(bf16[1,512,4096]{2,1,0:T(8,128)(2,1)} %param.7) | data formatting | bytes 8388608 | tf_op args[1]
  12.9 6.9 %copy.61 = f32[512,2,16,128]{3,0,2,1:T(8,128)} copy(bf16[512,2,16,128]{0,3,2,1:T(8,128)(2,1)} %bitcast.70) | data formatting | bytes 12582912 | tf_op jit(solution)/shard_map/convert_element_type | solution.py:25
  19.8 5.9 %multiply_convert_fusion = bf16[512,2,16,128]{3,0,2,1:T(8,128)(2,1)} fusion(f32[512,2,16,128]{3,0,2,1:T(8,128)} %copy.61), kind=kLoop, calls=%fused_computation.9 | loop fusion | flops 10485760 | bytes 12582912 | tf_op jit(solution)/shard_map/convert_element_type | solution.py:25
  25.7 5.6 %all-to-all-start.1 = ((bf16[512,2,16,128]{3,0,2,1:T(8,128)(2,1)}), bf16[512,2,16,128]{3,0,2,1:T(8,128)(2,1)}, u32[]{:S(2)}, u32[]{:S(2)}) async-start(bf16[512,2,16,128]{3,0,2,1:T(8,128)(2,1)} %multiply_convert_fusion), calls=%async_computation.1 | async-start | bytes 8388608 | tf_op jit(solution)/shard_map/all_to_all | solution.py:76
  31.3 6.4 %copy.62 = bf16[1,512,4096]{1,2,0:T(8,128)(2,1)} copy(bf16[1,512,4096]{2,1,0:T(8,128)(2,1)} %param.8) | data formatting | bytes 8388608 | tf_op args[2]
  37.7 6.2 %copy.63 = bf16[512,2,16,128]{3,0,2,1:T(8,128)(2,1)} copy(bf16[512,2,16,128]{0,3,2,1:T(8,128)(2,1)} %bitcast.72) | data formatting | bytes 8388608 | tf_op jit(solution)/shard_map/reshape;squeeze | solution.py:68
  43.9 34.2 %all-to-all-done.1 = bf16[512,2,16,128]{3,0,2,1:T(8,128)(2,1)} async-done(((bf16[512,2,16,128]{3,0,2,1:T(8,128)(2,1)}), bf16[512,2,16,128]{3,0,2,1:T(8,128)(2,1)}, u32[]{:S(2)}, u32[]{:S(2)}) %all-to-all-start.1) | async-done | bytes 4194336 | tf_op jit(solution)/shard_map/all_to_all | solution.py:76
  78.1 50.0 %all_to_all.54 = bf16[512,2,16,128]{3,0,2,1:T(8,128)(2,1)S(1)} all-to-all(bf16[512,2,16,128]{3,0,2,1:T(8,128)(2,1)} %copy.63), channel_id=1, replica_groups=mesh['head'=2,'seq'=16] {'head'}, dimensions={1} | all-to-all | bytes 8388608 | tf_op jit(solution)/shard_map/all_to_all | solution.py:77
  128.1 6.1 %fusion.20 = (f32[16,128,128]{2,1,0:T(8,128)}, f32[2,16,128,128]{3,2,1,0:T(8,128)S(1)}) fusion(bf16[512,2,16,128]{3,0,2,1:T(8,128)(2,1)S(1)} %all_to_all.54, bf16[512,2,16,128]{3,0,2,1:T(8,128)(2,1)} %all-to-all-done.1), kind=kOutput, calls=%fused_computation.27 | convolution fusion | flops 537133056 | bytes 11534336 | tf_op jit(solution)/shard_map/nbhd,nbhe->nhde/dot_general | solution.py:41
  134.2 6.4 %copy.56 = bf16[1,512,4096]{1,2,0:T(8,128)(2,1)} copy(bf16[1,512,4096]{2,1,0:T(8,128)(2,1)} %param.6) | data formatting | bytes 8388608 | tf_op args[0]
  140.6 7.1 %copy.58 = f32[512,2,16,128]{3,0,2,1:T(8,128)} copy(bf16[512,2,16,128]{0,3,2,1:T(8,128)(2,1)} %bitcast.71) | data formatting | bytes 12582912 | tf_op jit(solution)/shard_map/convert_element_type | solution.py:25
  147.7 5.9 %multiply_convert_fusion.1 = bf16[512,2,16,128]{3,0,2,1:T(8,128)(2,1)} fusion(f32[512,2,16,128]{3,0,2,1:T(8,128)} %copy.58), kind=kLoop, calls=%fused_computation.10 | loop fusion | flops 10485760 | bytes 12582912 | tf_op jit(solution)/shard_map/convert_element_type | solution.py:25
  153.6 5.6 %all-to-all-start = ((bf16[512,2,16,128]{3,0,2,1:T(8,128)(2,1)}), bf16[512,2,16,128]{3,0,2,1:T(8,128)(2,1)}, u32[]{:S(2)}, u32[]{:S(2)}) async-start(bf16[512,2,16,128]{3,0,2,1:T(8,128)(2,1)} %multiply_convert_fusion.1), calls=%async_computation | async-start | bytes 8388608 | tf_op jit(solution)/shard_map/all_to_all | solution.py:75
  160.5 43.8 %all-to-all-done = bf16[512,2,16,128]{3,0,2,1:T(8,128)(2,1)} async-done(((bf16[512,2,16,128]{3,0,2,1:T(8,128)(2,1)}), bf16[512,2,16,128]{3,0,2,1:T(8,128)(2,1)}, u32[]{:S(2)}, u32[]{:S(2)}) %all-to-all-start) | async-done | bytes 4194336 | tf_op jit(solution)/shard_map/all_to_all | solution.py:75
  204.3 13.9 %fusion.2 = f32[2,16,512,128]{3,2,1,0:T(8,128)} fusion(pred[512,512]{1,0:T(8,128)(4,1)S(1)} %iota_compare_fusion, bf16[512,2,16,128]{3,0,2,1:T(8,128)(2,1)} %all-to-all-done, bf16[512,2,16,128]{3,0,2,1:T(8,128)(2,1)} %copy-done, bf16[512,2,16,128]{3,0,2,1:T(8,128)(2,1)} %all-to-all-done.1), kind=kOutput, calls=%fused_computation.11 | convolution fusion | flops 4311744512 | bytes 21233664 | tf_op jit(solution)/shard_map/nhij,njhe->nihe/dot_general | solution.py:51
  218.2 41.8 %all-gather.3.cloned.1.call-done = f32[256,128,128]{2,1,0:T(8,128)} async-done(((f32[16,128,128]{2,1,0:T(8,128)}), f32[256,128,128]{2,1,0:T(8,128)}) %all-gather.3.cloned.1.call-update) | async-done | bytes 16777232 | tf_op jit(solution)/shard_map/all_gather | solution.py:15
  260.1 22.9 %while.10 = (s32[]{:T(128)}, f32[16,128,128]{2,1,0:T(8,128)S(1)}, s32[]{:T(128)}, f32[16,16,128,128]{3,2,1,0:T(8,128)}, s32[]{:T(128)}, /*index=5*/s32[]{:T(128)}, s32[]{:T(128)}) while((s32[]{:T(128)}, f32[16,128,128]{2,1,0:T(8,128)S(1)}, s32[]{:T(128)}, f32[16,16,128,128]{3,2,1,0:T(8,128)}, s32[]{:T(128)}, /*index=5*/s32[]{:T(128)}, ...), condition=%wide.region_2.3_spmd, body=%wide.region_1.2_spmd.sunk | while | flops 262149 | bytes 3145843 | solution.py:21
  283.1 9.1 %multiply_reduce_fusion = (f32[2,512,16]{1,2,0:T(8,128)S(1)}, f32[2,512,16,128]{3,1,2,0:T(8,128)S(1)}) fusion(bf16[512,2,16,128]{3,0,2,1:T(8,128)(2,1)} %all-to-all-done, f32[1,16,128,128]{3,2,1,0:T(8,128)S(1)} %slice.4, f32[16,128,128]{2,1,0:T(8,128)S(1)} %get-tuple-element.28, f32[2,16,512,128]{3,2,1,0:T(8,128)} %fusion.2), kind=kOutput, calls=%fused_computation.8 | convolution fusion | flops 3228024832 | bytes 23134208 | tf_op jit(solution)/shard_map/nihd,nhde->nihe/dot_general | solution.py:52
  292.1 8.1 %copy.67 = f32[2,512,16,128]{3,2,1,0:T(8,128)} copy(f32[2,512,16,128]{3,1,2,0:T(8,128)S(1)} %get-tuple-element.40) | data formatting | bytes 16777216 | tf_op jit(solution)/shard_map/add | solution.py:55
  300.4 5.2 %fusion.1 = bf16[1024,1,16,128]{3,2,0,1:T(8,128)(2,1)S(1)} fusion(f32[2,512,16,128]{3,2,1,0:T(8,128)} %copy.67, f32[1024,16]{1,0:T(8,128)S(1)} %bitcast.73), kind=kLoop, calls=%fused_computation.6 | loop fusion | flops 4194304 | bytes 12648448 | tf_op jit(solution)/shard_map/convert_element_type | solution.py:57
  305.6 49.5 %all_to_all.55 = bf16[1024,1,16,128]{3,2,1,0:T(8,128)(2,1)S(1)} all-to-all(bf16[1024,1,16,128]{3,2,1,0:T(8,128)(2,1)S(1)} %bitcast.68), channel_id=1, replica_groups=mesh['head'=2,'seq'=16] {'head'}, dimensions={0} | all-to-all | bytes 8388608 | tf_op jit(solution)/shard_map/all_to_all | solution.py:81
  359.0 10.0 %copy.72 = f32[512,2,1,16,128]{0,4,3,1,2:T(8,128)} copy(f32[512,2,1,16,128]{4,3,0,1,2:T(8,128)} %convert_bitcast_fusion) | data formatting | bytes 16777216 | tf_op jit(solution)/shard_map/convert_element_type | solution.py:83
  369.0 5.1 %fusion = bf16[1,512,4096]{1,2,0:T(8,128)(2,1)} fusion(f32[512,2,1,16,128]{0,4,3,1,2:T(8,128)} %copy.72, f32[4096]{0:T(1024)S(1)} %copy-done.1), kind=kLoop, calls=%fused_computation.4 | loop fusion | flops 4194304 | bytes 12599296 | tf_op jit(solution)/shard_map/convert_element_type | solution.py:83
  374.2 6.3 %copy.73 = bf16[1,512,4096]{2,1,0:T(8,128)(2,1)} copy(bf16[1,512,4096]{1,2,0:T(8,128)(2,1)} %fusion) | data formatting | bytes 8388608 | tf_op jit(solution)/shard_map/convert_element_type | solution.py:83
  (28 shorter events, 27.8 us)
Async XLA Ops:
  25.7 52.4 %all-to-all-start.1 = ((bf16[512,2,16,128]{3,0,2,1:T(8,128)(2,1)}), bf16[512,2,16,128]{3,0,2,1:T(8,128)(2,1)}, u32[]{:S(2)}, u32[]{:S(2)}) async-start(bf16[512,2,16,128]{3,0,2,1:T(8,128)(2,1)} %multiply_convert_fusion), calls=%async_computation.1 | async-start | bytes 8388608 | tf_op jit(solution)/shard_map/all_to_all | solution.py:76
  31.3 228.8 %all-gather.3.cloned.1.call-start = ((), (), s32[]{:S(2)}) async-start(), calls=%async_computation.4 | async-start | bytes 17825792 | tf_op jit(solution)/shard_map/all_gather | solution.py:15
  128.1 6.1 %copy-start = (bf16[512,2,16,128]{3,0,2,1:T(8,128)(2,1)}, bf16[512,2,16,128]{3,0,2,1:T(8,128)(2,1)S(1)}, u32[]{:S(2)}) copy-start(bf16[512,2,16,128]{3,0,2,1:T(8,128)(2,1)S(1)} %all_to_all.54) | copy-start | bytes 12582916
  153.6 50.7 %all-to-all-start = ((bf16[512,2,16,128]{3,0,2,1:T(8,128)(2,1)}), bf16[512,2,16,128]{3,0,2,1:T(8,128)(2,1)}, u32[]{:S(2)}, u32[]{:S(2)}) async-start(bf16[512,2,16,128]{3,0,2,1:T(8,128)(2,1)} %multiply_convert_fusion.1), calls=%async_computation | async-start | bytes 8388608 | tf_op jit(solution)/shard_map/all_to_all | solution.py:75
  359.0 10.0 %copy-start.1 = (f32[4096]{0:T(1024)S(1)}, f32[4096]{0:T(1024)}, u32[]{:S(2)}) copy-start(f32[4096]{0:T(1024)} %param.9) | copy-start | bytes 49156
Sparse Core Ops, SparseCore 0:
  134.3 125.6 all-gather.2
where the time goes:
time: 389 us; the launch traced here: 387 us
  waiting for transfers between devices  120 us (31%)
  blocking collectives  99.5 us (26%)
  local copies, waits for them, and re-layouts  64.1 us (16%)
  other arithmetic  49.5 us (13%)
  matrix products  29.1 us (7%)
  between operations  13.5 us (3%)
  starting transfers between devices  11.3 us (3%)
    all_to_all x1, blocking collectives, local(): lax.all_to_all(plain_v, 'head', split_axis=1, concat_axis=0, tiled=True)  50 us
    all_to_all x1, blocking collectives, local(): lax.all_to_all(normed, 'head', split_axis=0, concat_axis=1, tiled=True)  49.5 us
    all_to_all x1, waiting for transfers between devices, local(): lax.all_to_all(act_q, 'head', split_axis=1, concat_axis=0, tiled=True)  43.8 us
    all_gather x1, waiting for transfers between devices, prefix_2(): gathered = lax.all_gather(part, axis)  41.8 us
    all_to_all x1, waiting for transfers between devices, local(): lax.all_to_all(act_k, 'head', split_axis=1, concat_axis=0, tiled=True)  34.2 us
    add x15, other arithmetic, add_states(): return earlier + later  22.3 us
    unnamed x7, local copies, waits for them, and re-layouts  19.2 us
    convert_element_type x2, local copies, waits for them, and re-layouts, activate(): return jax.nn.silu(rows.astype(jnp.float32)).astype(jnp.bfloat16)  14 us
  transfers between devices with their start and end apart: 3, of which 3 were waited for; matrix products, arithmetic and copies ran while one was open for 12% of the time, Pallas kernels for 0%

commit v1 on v0

v1 whole, which is shorter than its diff:
```python
import functools

import jax
import jax.numpy as jnp
from jax import lax
from jax.experimental import pallas as pl
from jax.experimental.pallas import tpu as pltpu
from jax.sharding import PartitionSpec as P

DH = 128
EPS = 1e-06
MESH = pl.DeviceIdType.MESH


def silu(rows):
    x = rows.astype(jnp.float32)
    half = x * 0.5
    return (half + half * jnp.tanh(half)).astype(jnp.bfloat16)


def kernel(inner, outer, groups, q_hbm, k_hbm, v_hbm, gain_ref, out_hbm, q, k, v, o_local, o, kv_out, kv_in, pre, tot_out, tot_in,
           pre_out, pre_in, load_sem, store_sem, s1, r1, s2, r2, s3, r3):
    members = inner * groups
    rows = q.shape[0]
    chunks = kv_in.shape[0]
    wide = members * DH
    seq, grp = lax.axis_index("seq"), lax.axis_index("head")
    plane = seq // inner
    me = (seq % inner) * groups + grp

    def device(z, j):
        return {"seq": z * inner + j // groups, "head": j % groups}

    def peer(r):
        return lax.rem(me + r, members)

    def cols(c, j):
        return pl.ds(pl.multiple_of((c * members + j) * DH, DH), DH)

    def load(n, c):
        src, dst = ((k_hbm, k), (v_hbm, v), (q_hbm, q))[n]
        where = pl.ds(c * wide, wide)
        return pltpu.make_async_copy(src.at[0, :, where], dst.at[:, where], load_sem.at[n, c])

    def store(c):
        where = pl.ds(c * wide, wide)
        return pltpu.make_async_copy(o.at[:, where], out_hbm.at[0, :, where], store_sem.at[c])

    def copy1(c, to, frm):
        return pltpu.make_async_remote_copy(kv_out.at[c, to], kv_in.at[c, frm], s1.at[c, to], r1.at[c, frm],
                                            device_id=device(plane, to), device_id_type=MESH)

    def copy2(c, to, frm):
        return pltpu.make_async_remote_copy(tot_out.at[c], tot_in.at[c, frm], s2.at[c, to], r2.at[c, frm],
                                            device_id=device(to, me), device_id_type=MESH)

    def copy3(c, to, frm):
        return pltpu.make_async_remote_copy(pre_out.at[c, to], pre_in.at[c, frm], s3.at[c, to], r3.at[c, frm],
                                            device_id=device(plane, to), device_id_type=MESH)

    barrier = pltpu.get_barrier_semaphore()

    @pl.loop(1, members)
    def _(r):
        pl.semaphore_signal(barrier, inc=1, device_id=device(plane, peer(r)), device_id_type=MESH)

    @pl.loop(1, outer)
    def _(r):
        pl.semaphore_signal(barrier, inc=1, device_id=device(lax.rem(plane + r, outer), me), device_id_type=MESH)

    for c in range(chunks):
        load(0, c).start()
        load(1, c).start()
    for c in range(chunks):
        load(2, c).start()

    pl.semaphore_wait(barrier, members + outer - 2)

    def state(c, j):
        where = cols(c, j)
        ka = silu(k[:, where])
        k[:, where] = ka
        return lax.dot_general(ka, v[:, where], (((0,), (0,)), ((), ())), preferred_element_type=jnp.float32)

    def states(c):
        load(0, c).wait()
        load(1, c).wait()

        @pl.loop(1, members)
        def _(r):
            to = peer(r)
            kv_out[c, to] = state(c, to).astype(jnp.bfloat16)
            copy1(c, to, me).start()

        kv_in[c, me] = state(c, me).astype(jnp.bfloat16)

    def totals(c):
        @pl.loop(1, members)
        def _(r):
            frm = peer(r)
            copy1(c, frm, frm).wait_recv()

        def one(i, run):
            pre[c, i] = run
            return run + kv_in[c, i].astype(jnp.float32)

        run = lax.fori_loop(0, members, one, jnp.zeros((DH, DH), jnp.float32))
        tot_out[c] = run.astype(jnp.bfloat16)

        @pl.loop(plane + 1, outer)
        def _(to):
            copy2(c, to, plane).start()

    def prefixes(c):
        def one(frm, run):
            copy2(c, frm, frm).wait_recv()
            return run + tot_in[c, frm].astype(jnp.float32)

        base = lax.fori_loop(0, plane, one, jnp.zeros((DH, DH), jnp.float32))

        @pl.loop(1, members)
        def _(r):
            to = peer(r)
            pre_out[c, to] = (base + pre[c, to]).astype(jnp.bfloat16)
            copy3(c, to, me).start()

        pre_in[c, me] = (base + pre[c, me]).astype(jnp.bfloat16)

    tile = rows // 2 if rows % 512 == 0 else rows
    causal = lax.broadcasted_iota(jnp.int32, (tile, tile), 0) >= lax.broadcasted_iota(jnp.int32, (tile, tile), 1)

    def scores_of(a, b):
        return lax.dot_general(a, b, (((1,), (1,)), ((), ())), preferred_element_type=jnp.float32)

    def local(c):
        load(2, c).wait()

        @pl.loop(0, members)
        def _(j):
            where = cols(c, j)
            qa = silu(q[:, where])
            q[:, where] = qa
            for i in range(rows // tile):
                q_i = qa[i * tile:(i + 1) * tile]
                k_i = k[i * tile:(i + 1) * tile, where]
                s = jnp.where(causal, scores_of(q_i, k_i), 0.0).astype(jnp.bfloat16)
                part = jnp.dot(s, v[i * tile:(i + 1) * tile, where], preferred_element_type=jnp.float32)
                if i > 0:
                    s = scores_of(q_i, k[:i * tile, where]).astype(jnp.bfloat16)
                    part = part + jnp.dot(s, v[:i * tile, where], preferred_element_type=jnp.float32)
                o_local[i * tile:(i + 1) * tile, where] = part

    def finish(c):
        @pl.loop(0, members)
        def _(j):
            where = cols(c, j)

            @pl.when(j != me)
            def _():
                copy3(c, j, j).wait_recv()

            r = o_local[:, where] + jnp.dot(q[:, where], pre_in[c, j], preferred_element_type=jnp.float32)
            normed = r * lax.rsqrt(jnp.mean(r * r, axis=-1, keepdims=True) + EPS)
            normed = normed.astype(jnp.bfloat16).astype(jnp.float32)
            o[:, where] = (normed * gain_ref[:, where]).astype(jnp.bfloat16)

        store(c).start()

    for c in range(chunks):
        states(c)
    for c in range(chunks):
        totals(c)
        local(c)
        if c > 0:
            prefixes(c - 1)
    prefixes(chunks - 1)
    for c in range(chunks):
        finish(c)
    for c in range(chunks):
        store(c).wait()

        @pl.loop(1, members)
        def _(r):
            to = peer(r)
            copy1(c, to, me).wait_send()
            copy3(c, to, me).wait_send()

        @pl.loop(plane + 1, outer)
        def _(to):
            copy2(c, to, plane).wait_send()


def solution(mesh):
    span_parts, groups = mesh.shape["seq"], mesh.shape["head"]

    def local(queries, key_rows, value_rows, head_gain):
        rows, features = queries.shape[1:]
        heads = features // DH
        inner = 1
        while (4 * inner * inner <= span_parts and span_parts % (2 * inner) == 0
               and heads % (2 * inner * groups) == 0):
            inner *= 2
        outer = span_parts // inner
        members = inner * groups
        chunks = heads // members
        bf, f4, dma = jnp.bfloat16, jnp.float32, pltpu.SemaphoreType.DMA
        anywhere = pl.BlockSpec(memory_space=pl.ANY)
        return pl.pallas_call(
            functools.partial(kernel, inner, outer, groups),
            out_shape=jax.ShapeDtypeStruct(queries.shape, bf),
            in_specs=[anywhere] * 3 + [pl.BlockSpec(memory_space=pltpu.VMEM)],
            out_specs=anywhere,
            scratch_shapes=[
                pltpu.VMEM((rows, features), bf),
                pltpu.VMEM((rows, features), bf),
                pltpu.VMEM((rows, features), bf),
                pltpu.VMEM((rows, features), f4),
                pltpu.VMEM((rows, features), bf),
                pltpu.VMEM((chunks, members, DH, DH), bf),
                pltpu.VMEM((chunks, members, DH, DH), bf),
                pltpu.VMEM((chunks, members, DH, DH), f4),
                pltpu.VMEM((chunks, DH, DH), bf),
                pltpu.VMEM((chunks, outer, DH, DH), bf),
                pltpu.VMEM((chunks, members, DH, DH), bf),
                pltpu.VMEM((chunks, members, DH, DH), bf),
                dma((3, chunks)),
                dma((chunks,)),
                dma((chunks, members)),
                dma((chunks, members)),
                dma((chunks, outer)),
                dma((chunks, outer)),
                dma((chunks, members)),
                dma((chunks, members)),
            ],
            compiler_params=pltpu.CompilerParams(
                collective_id=0, has_side_effects=True, vmem_limit_bytes=60 * 1024 * 1024
            ),
            name="scan_attention",
        )(queries, key_rows, value_rows, head_gain.reshape(1, features))

    placed = (P("seq", "head", None),) * 3 + (P(),)
    return jax.shard_map(local, mesh=mesh, in_specs=placed, out_specs=P("seq", "head", None), check_vma=False)
```

time: 389 us -> 51.2 us (0.13)
  the two profiles are of different devices: /device:TPU:27 before, /device:TPU:0 now
where the time goes in v1:
time: 51.2 us; the launch traced here: 51 us
  Pallas kernels  46.2 us (90%)
  local copies, waits for them, and re-layouts  4.7 us (9%)
    pallas_call x1, Pallas kernels, local(): pl.pallas_call(functools.partial(kernel, inner, outer, groups), out_shape...  46.2 us
    unnamed x1, local copies, waits for them, and re-layouts  4.7 us

profile of v1, /device:TPU:0, one launch (start us, length us, event | category | flops | bytes accessed | tf_op | source)
XLA Modules:
  0.0 51.0 jit_solution(15364701769801604841)
XLA Ops:
  0.0 46.2 %scan_attention.1 = bf16[1,512,4096]{2,1,0:T(8,128)(2,1)} custom-call(bf16[1,512,4096]{2,1,0:T(8,128)(2,1)} %q_hbm.1, bf16[1,512,4096]{2,1,0:T(8,128)(2,1)} %k_hbm.1, bf16[1,512,4096]{2,1,0:T(8,128)(2,1)} %v_hbm.1, f32[1,4096]{1,0:T(1,128)} %bitcast.1), custom_call_target="tpu_custom_call" | custom-call | tf_op jit(solution)/shard_map/scan_attention/pallas_call | solution.py:208
  46.3 4.7 %copy.6 = bf16[1,512,4096]{2,1,0:T(8,128)(2,1)} copy(bf16[1,512,4096]{2,1,0:T(8,128)(2,1)} %scan_attention.1) | data formatting | bytes 8388608

commit v2 on v1

--- a/solution.py
+++ b/solution.py
@@ -18,12 +18,13 @@
     return (half + half * jnp.tanh(half)).astype(jnp.bfloat16)
 
 
-def kernel(inner, outer, groups, q_hbm, k_hbm, v_hbm, gain_ref, out_hbm, q, k, v, o_local, o, kv_out, kv_in, pre, tot_out, tot_in,
+def kernel(inner, outer, groups, q_hbm, k_hbm, v_hbm, gain_ref, out_hbm, q, k, v, k_t, earlier, o, kv_out, kv_in, pre, tot_out, tot_in,
            pre_out, pre_in, load_sem, store_sem, s1, r1, s2, r2, s3, r3):
     members = inner * groups
-    rows = q.shape[0]
+    blocks = q.shape[0] // DH
     chunks = kv_in.shape[0]
     wide = members * DH
+    unroll = 2 if members % 2 == 0 else 1
     seq, grp = lax.axis_index("seq"), lax.axis_index("head")
     plane = seq // inner
     me = (seq % inner) * groups + grp
@@ -33,9 +34,6 @@
 
     def peer(r):
         return lax.rem(me + r, members)
-
-    def cols(c, j):
-        return pl.ds(pl.multiple_of((c * members + j) * DH, DH), DH)
 
     def load(n, c):
         src, dst = ((k_hbm, k), (v_hbm, v), (q_hbm, q))[n]
@@ -76,23 +74,42 @@
 
     pl.semaphore_wait(barrier, members + outer - 2)
 
-    def state(c, j):
-        where = cols(c, j)
-        ka = silu(k[:, where])
-        k[:, where] = ka
-        return lax.dot_general(ka, v[:, where], (((0,), (0,)), ((), ())), preferred_element_type=jnp.float32)
+    def pick(j, b):
+        return pl.ds(b * DH, DH), cols_of(j)
+
+    def cols_of(h):
+        return pl.ds(pl.multiple_of(h * DH, DH), DH)
+
+    def state(h):
+        run = None
+        for b in range(blocks):
+            where = pick(h, b)
+            kt = silu(k[where]).T
+            k_t[h, b] = kt
+            part = jnp.dot(kt, v[where], preferred_element_type=jnp.float32)
+            if b > 0:
+                earlier[h, b - 1] = run
+            run = part if b == 0 else run + part
+        return run.astype(jnp.bfloat16)
 
     def states(c):
         load(0, c).wait()
         load(1, c).wait()
 
-        @pl.loop(1, members)
-        def _(r):
-            to = peer(r)
-            kv_out[c, to] = state(c, to).astype(jnp.bfloat16)
-            copy1(c, to, me).start()
-
-        kv_in[c, me] = state(c, me).astype(jnp.bfloat16)
+        @pl.loop(0, members // unroll)
+        def _(step):
+            tos = [peer(step * unroll + u + 1) for u in range(unroll)]
+            made = [state(c * members + to) for to in tos]
+            for to, one in zip(tos, made):
+                kv_out[c, to] = one
+
+                @pl.when(to != me)
+                def _():
+                    copy1(c, to, me).start()
+
+                @pl.when(to == me)
+                def _():
+                    kv_in[c, me] = one
 
     def totals(c):
         @pl.loop(1, members)
@@ -126,43 +143,46 @@
 
         pre_in[c, me] = (base + pre[c, me]).astype(jnp.bfloat16)
 
-    tile = rows // 2 if rows % 512 == 0 else rows
-    causal = lax.broadcasted_iota(jnp.int32, (tile, tile), 0) >= lax.broadcasted_iota(jnp.int32, (tile, tile), 1)
-
-    def scores_of(a, b):
-        return lax.dot_general(a, b, (((1,), (1,)), ((), ())), preferred_element_type=jnp.float32)
+    causal = lax.broadcasted_iota(jnp.int32, (DH, DH), 0) >= lax.broadcasted_iota(jnp.int32, (DH, DH), 1)
 
     def local(c):
         load(2, c).wait()
 
-        @pl.loop(0, members)
-        def _(j):
-            where = cols(c, j)
-            qa = silu(q[:, where])
-            q[:, where] = qa
-            for i in range(rows // tile):
-                q_i = qa[i * tile:(i + 1) * tile]
-                k_i = k[i * tile:(i + 1) * tile, where]
-                s = jnp.where(causal, scores_of(q_i, k_i), 0.0).astype(jnp.bfloat16)
-                part = jnp.dot(s, v[i * tile:(i + 1) * tile, where], preferred_element_type=jnp.float32)
-                if i > 0:
-                    s = scores_of(q_i, k[:i * tile, where]).astype(jnp.bfloat16)
-                    part = part + jnp.dot(s, v[:i * tile, where], preferred_element_type=jnp.float32)
-                o_local[i * tile:(i + 1) * tile, where] = part
+        @pl.loop(0, members // unroll)
+        def _(step):
+            for u in range(unroll):
+                h = c * members + step * unroll + u
+                for b in range(blocks):
+                    where = pick(h, b)
+                    qa = silu(q[where])
+                    q[where] = qa
+                    s = jnp.dot(qa, k_t[h, b], preferred_element_type=jnp.float32)
+                    k[where] = jnp.where(causal, s, 0.0).astype(jnp.bfloat16)
 
     def finish(c):
-        @pl.loop(0, members)
-        def _(j):
-            where = cols(c, j)
-
-            @pl.when(j != me)
-            def _():
-                copy3(c, j, j).wait_recv()
-
-            r = o_local[:, where] + jnp.dot(q[:, where], pre_in[c, j], preferred_element_type=jnp.float32)
-            normed = r * lax.rsqrt(jnp.mean(r * r, axis=-1, keepdims=True) + EPS)
-            normed = normed.astype(jnp.bfloat16).astype(jnp.float32)
-            o[:, where] = (normed * gain_ref[:, where]).astype(jnp.bfloat16)
+        @pl.loop(0, members // unroll)
+        def _(step):
+            js = [step * unroll + u for u in range(unroll)]
+            for j in js:
+                @pl.when(j != me)
+                def _():
+                    copy3(c, j, j).wait_recv()
+
+            for j in js:
+                h = c * members + j
+                prefix = pre_in[c, j]
+                wide_prefix = prefix.astype(jnp.float32)
+                gain = gain_ref[:, cols_of(h)]
+                for b in range(blocks):
+                    where = pick(h, b)
+                    if b > 0:
+                        prefix = (wide_prefix + earlier[h, b - 1]).astype(jnp.bfloat16)
+                    left = jnp.concatenate([k[where], q[where]], axis=1)
+                    right = jnp.concatenate([v[where], prefix], axis=0)
+                    r = jnp.dot(left, right, preferred_element_type=jnp.float32)
+                    normed = r * lax.rsqrt(jnp.mean(r * r, axis=-1, keepdims=True) + EPS)
+                    normed = normed.astype(jnp.bfloat16).astype(jnp.float32)
+                    o[where] = (normed * gain).astype(jnp.bfloat16)
 
         store(c).start()
 
@@ -195,7 +215,7 @@
 
     def local(queries, key_rows, value_rows, head_gain):
         rows, features = queries.shape[1:]
-        heads = features // DH
+        heads, blocks = features // DH, rows // DH
         inner = 1
         while (4 * inner * inner <= span_parts and span_parts % (2 * inner) == 0
                and heads % (2 * inner * groups) == 0):
@@ -214,7 +234,8 @@
                 pltpu.VMEM((rows, features), bf),
                 pltpu.VMEM((rows, features), bf),
                 pltpu.VMEM((rows, features), bf),
-                pltpu.VMEM((rows, features), f4),
+                pltpu.VMEM((heads, blocks, DH, DH), bf),
+                pltpu.VMEM((heads, max(blocks - 1, 1), DH, DH), f4),
                 pltpu.VMEM((rows, features), bf),
                 pltpu.VMEM((chunks, members, DH, DH), bf),
                 pltpu.VMEM((chunks, members, DH, DH), bf),

time: 51.2 us -> 40.6 us (0.79)
  Pallas kernels: 46.2 us -> 35.6 us
    pallas_call x1, Pallas kernels: 46.2 us -> 35.6 us  [local(): pl.pallas_call(functools.partial(kernel, inner, outer, groups), out_shape...]
where the time goes in v2:
time: 40.6 us; the launch traced here: 40.3 us
  Pallas kernels  35.6 us (88%)
  local copies, waits for them, and re-layouts  4.7 us (12%)
    pallas_call x1, Pallas kernels, local(): pl.pallas_call(functools.partial(kernel, inner, outer, groups), out_shape...  35.6 us
    unnamed x1, local copies, waits for them, and re-layouts  4.7 us

profile of v2, /device:TPU:0, one launch (start us, length us, event | category | flops | bytes accessed | tf_op | source)
XLA Modules:
  0.0 40.3 jit_solution(11663047720212152824)
XLA Ops:
  0.0 35.6 %scan_attention.1 = bf16[1,512,4096]{2,1,0:T(8,128)(2,1)} custom-call(bf16[1,512,4096]{2,1,0:T(8,128)(2,1)} %q_hbm.1, bf16[1,512,4096]{2,1,0:T(8,128)(2,1)} %k_hbm.1, bf16[1,512,4096]{2,1,0:T(8,128)(2,1)} %v_hbm.1, f32[1,4096]{1,0:T(1,128)} %bitcast.1), custom_call_target="tpu_custom_call" | custom-call | tf_op jit(solution)/shard_map/scan_attention/pallas_call | solution.py:228
  35.6 4.7 %copy.6 = bf16[1,512,4096]{2,1,0:T(8,128)(2,1)} copy(bf16[1,512,4096]{2,1,0:T(8,128)(2,1)} %scan_attention.1) | data formatting | bytes 8388608

commit v3 on v2

--- a/solution.py
+++ b/solution.py
@@ -18,8 +18,8 @@
     return (half + half * jnp.tanh(half)).astype(jnp.bfloat16)
 
 
-def kernel(inner, outer, groups, q_hbm, k_hbm, v_hbm, gain_ref, out_hbm, q, k, v, k_t, earlier, o, kv_out, kv_in, pre, tot_out, tot_in,
-           pre_out, pre_in, load_sem, store_sem, s1, r1, s2, r2, s3, r3):
+def kernel(inner, outer, groups, q_hbm, k_hbm, v_hbm, gain_ref, o, q, k, v, k_t, earlier, kv_out, kv_in, pre, tot_out, tot_in,
+           pre_out, pre_in, load_sem, s1, r1, s2, r2, s3, r3):
     members = inner * groups
     blocks = q.shape[0] // DH
     chunks = kv_in.shape[0]
@@ -39,10 +39,6 @@
         src, dst = ((k_hbm, k), (v_hbm, v), (q_hbm, q))[n]
         where = pl.ds(c * wide, wide)
         return pltpu.make_async_copy(src.at[0, :, where], dst.at[:, where], load_sem.at[n, c])
-
-    def store(c):
-        where = pl.ds(c * wide, wide)
-        return pltpu.make_async_copy(o.at[:, where], out_hbm.at[0, :, where], store_sem.at[c])
 
     def copy1(c, to, frm):
         return pltpu.make_async_remote_copy(kv_out.at[c, to], kv_in.at[c, frm], s1.at[c, to], r1.at[c, frm],
@@ -162,7 +158,7 @@
     def finish(c):
         @pl.loop(0, members // unroll)
         def _(step):
-            js = [step * unroll + u for u in range(unroll)]
+            js = [lax.rem(me - step * unroll - u + members, members) for u in range(unroll)]
             for j in js:
                 @pl.when(j != me)
                 def _():
@@ -184,8 +180,6 @@
                     normed = normed.astype(jnp.bfloat16).astype(jnp.float32)
                     o[where] = (normed * gain).astype(jnp.bfloat16)
 
-        store(c).start()
-
     for c in range(chunks):
         states(c)
     for c in range(chunks):
@@ -197,8 +191,6 @@
     for c in range(chunks):
         finish(c)
     for c in range(chunks):
-        store(c).wait()
-
         @pl.loop(1, members)
         def _(r):
             to = peer(r)
@@ -225,18 +217,17 @@
         chunks = heads // members
         bf, f4, dma = jnp.bfloat16, jnp.float32, pltpu.SemaphoreType.DMA
         anywhere = pl.BlockSpec(memory_space=pl.ANY)
-        return pl.pallas_call(
+        done = pl.pallas_call(
             functools.partial(kernel, inner, outer, groups),
-            out_shape=jax.ShapeDtypeStruct(queries.shape, bf),
+            out_shape=pltpu.VMEM((rows, features), bf),
             in_specs=[anywhere] * 3 + [pl.BlockSpec(memory_space=pltpu.VMEM)],
-            out_specs=anywhere,
+            out_specs=pl.BlockSpec(memory_space=pltpu.VMEM),
             scratch_shapes=[
                 pltpu.VMEM((rows, features), bf),
                 pltpu.VMEM((rows, features), bf),
                 pltpu.VMEM((rows, features), bf),
                 pltpu.VMEM((heads, blocks, DH, DH), bf),
                 pltpu.VMEM((heads, max(blocks - 1, 1), DH, DH), f4),
-                pltpu.VMEM((rows, features), bf),
                 pltpu.VMEM((chunks, members, DH, DH), bf),
                 pltpu.VMEM((chunks, members, DH, DH), bf),
                 pltpu.VMEM((chunks, members, DH, DH), f4),
@@ -245,7 +236,6 @@
                 pltpu.VMEM((chunks, members, DH, DH), bf),
                 pltpu.VMEM((chunks, members, DH, DH), bf),
                 dma((3, chunks)),
-                dma((chunks,)),
                 dma((chunks, members)),
                 dma((chunks, members)),
                 dma((chunks, outer)),
@@ -254,10 +244,11 @@
                 dma((chunks, members)),
             ],
             compiler_params=pltpu.CompilerParams(
-                collective_id=0, has_side_effects=True, vmem_limit_bytes=60 * 1024 * 1024
+                collective_id=0, has_side_effects=True, vmem_limit_bytes=56 * 1024 * 1024
             ),
             name="scan_attention",
         )(queries, key_rows, value_rows, head_gain.reshape(1, features))
+        return done.reshape(queries.shape)
 
     placed = (P("seq", "head", None),) * 3 + (P(),)
     return jax.shard_map(local, mesh=mesh, in_specs=placed, out_specs=P("seq", "head", None), check_vma=False)

time: 40.6 us -> 36 us (0.89)
  local copies, waits for them, and re-layouts: 4.7 us -> 2.02 us
  Pallas kernels: 35.6 us -> 33.8 us
    unnamed x1, local copies, waits for them, and re-layouts: 4.7 us -> 2.02 us
    pallas_call x1, Pallas kernels: 35.6 us -> 33.8 us  [local(): pl.pallas_call(functools.partial(kernel, inner, outer, groups), out_shape...]
where the time goes in v3:
time: 36 us; the launch traced here: 35.8 us
  Pallas kernels  33.8 us (94%)
  local copies, waits for them, and re-layouts  2.02 us (6%)
    pallas_call x1, Pallas kernels, local(): pl.pallas_call(functools.partial(kernel, inner, outer, groups), out_shape...  33.8 us
    unnamed x1, local copies, waits for them, and re-layouts  2.02 us

profile of v3, /device:TPU:0, one launch (start us, length us, event | category | flops | bytes accessed | tf_op | source)
XLA Modules:
  0.0 35.8 jit_solution(15817893917764348288)
XLA Ops:
  0.0 33.8 %scan_attention.1 = bf16[512,4096]{1,0:T(8,128)(2,1)S(1)} custom-call(bf16[1,512,4096]{2,1,0:T(8,128)(2,1)} %q_hbm.1, bf16[1,512,4096]{2,1,0:T(8,128)(2,1)} %k_hbm.1, bf16[1,512,4096]{2,1,0:T(8,128)(2,1)} %v_hbm.1, f32[1,4096]{1,0:T(1,128)} %bitcast.3), custom_call_target="tpu_custom_call" | custom-call | tf_op jit(solution)/shard_map/scan_attention/pallas_call | solution.py:220
  33.8 2.0 %copy.6 = bf16[1,512,4096]{2,1,0:T(8,128)(2,1)} copy(bf16[1,512,4096]{2,1,0:T(8,128)(2,1)S(1)} %bitcast.2) | data formatting | bytes 8388608
